TPU v7x, 512 devices: a whole 4x8x8 slice. The times are simulated.
512 devices in a mesh: seq: 64 (over z_hi, y, x), head: 8 (over z_lo, core).
Axes of the slice: x: 4, y: 8, z: 8 (z_hi: 2, z_lo: 4; z = z_hi * 4 + z_lo), core: 2. Of those that a mesh axis runs over, the one named last changes fastest.
Arguments:
- queries: bfloat16 [16384, 4096], P('seq', 'head'), may hold values from -6 to 6
- key_rows: bfloat16 [16384, 4096], P('seq', 'head'), may hold values from -6 to 6
- value_rows: bfloat16 [16384, 4096], P('seq', 'head'), may hold values from -180 to 180
- window: int32 [256, 12], P('seq'), may hold values from 0 to 255, as said below
- random_blocks: int32 [256, 3], P('seq'), may hold values from 0 to 255, as said below
- global_blocks: int32 [2], replicated, may hold values from 0 to 255, as said below
- norm_gain: float32 [4096], P('head'), may hold values from 0.25 to 1.75
Outputs:
- normed: bfloat16 [16384, 4096], P('seq', 'head')
Inputs may be any that keep to these rules, and one draw needn't show every extreme that they name: `window`: row b names 12 distinct blocks, each with (id - b) mod 256 within 8 of 0 either way around the circle; b itself, b - 8 and b + 8 (mod 256) are always among them. `random_blocks`: shard s holds blocks s * 4 to s * 4 + 3. The 12 entries of the rows of one device name each shard at most 1 times; one shard is named exactly 1 times by the rows of every device. `global_blocks`: distinct blocks; one of them is the last block of the sequence, 255.
All inputs are finite; a program needn't handle non-finite values.
Results may differ from a plain program's by a relative error of at most 0.0045.
Values may be sent and summed in bfloat16 or wider, within the bound.
A program may use at most 128 MiB of HBM per device.

v0:
```python
from functools import partial

import jax
import jax.numpy as jnp
from jax import lax
from jax.sharding import PartitionSpec as P

HD = 128
D = 4096
BLK = 64


def from_behind(shard, axis, by):
    peers = lax.axis_size(axis)
    return lax.ppermute(shard, axis, [(i, (i + by) % peers) for i in range(peers)])


def source_part(query_set, key_set, value_set, head_count):
    item_count, row_count, row_width = query_set.shape
    head_size = row_width // head_count
    query_heads = query_set.reshape(item_count, row_count, head_count, head_size)
    key_heads = key_set.reshape(item_count, key_set.shape[1], head_count, head_size)
    value_heads = value_set.reshape(item_count, value_set.shape[1], head_count, head_size)
    scores = jnp.einsum(
        "nqhd,nkhd->nhqk", query_heads, key_heads, preferred_element_type=jnp.float32
    ) * head_size ** (-0.5)
    maxima = jnp.max(scores, axis=-1)
    lifted = jnp.exp(scores - maxima[..., None])
    totals = jnp.sum(lifted, axis=-1)
    weights = lifted.astype(jnp.bfloat16)
    summed = jnp.einsum("nhqk,nkhd->nqhd", weights, value_heads, preferred_element_type=jnp.float32)
    return (maxima, totals, summed.reshape(item_count, row_count, row_width))


def merge_sources(maxima, totals, partial_sums, head_count):
    overall = jnp.max(maxima, axis=0)
    factor = jnp.exp(maxima - overall[None])
    denominator = jnp.sum(factor * totals, axis=0)
    item_count, row_count, row_width = partial_sums.shape
    split_sums = partial_sums.reshape(item_count, row_count, head_count, row_width // head_count)
    weighted = jnp.sum(split_sums * jnp.transpose(factor, (0, 2, 1))[..., None], axis=0)
    return (weighted / jnp.transpose(denominator)[..., None]).reshape(row_count, row_width)


def body(queries, key_rows, value_rows, window, random_blocks, global_blocks, norm_gain):
    per_device = window.shape[0]
    row_width = queries.shape[1]
    head_count = row_width // HD
    shards = lax.axis_size("seq")
    position = lax.axis_index("seq")
    stacked = jnp.stack([key_rows, value_rows])
    stacked_blocks = stacked.reshape(2, per_device, BLK, row_width)
    query_blocks = queries.reshape(per_device, BLK, row_width)
    fetched = {}
    for offset in (2, 1, -1, -2):
        fetched[offset] = from_behind(stacked, "seq", offset)
    beside_all = [fetched[2], fetched[1], stacked, fetched[-1], fetched[-2]]
    glob_owner = global_blocks // per_device
    glob_within = global_blocks % per_device
    own_copies = jnp.take(stacked_blocks, glob_within, axis=1).astype(jnp.float32)
    holder = (glob_owner == position)[None, :, None, None]
    masked = jnp.where(holder, own_copies, 0.0)
    global_kv = lax.psum(masked, "seq").astype(jnp.bfloat16)
    window_pool = jnp.stack(beside_all, axis=1).reshape(2, 5 * per_device, BLK, row_width)
    key_pool = jnp.concatenate([window_pool, global_kv], axis=1)
    local_index = (window // per_device - position + 2) % shards * per_device + window % per_device
    glob_index = 5 * per_device + jnp.arange(global_blocks.shape[0], dtype=jnp.int32)
    near_index = jnp.concatenate(
        [local_index, jnp.broadcast_to(glob_index[None, :], (per_device, glob_index.shape[0]))],
        axis=1,
    )

    def near_block(items):
        one_query, one_index = items
        near_keys = jnp.take(key_pool[0], one_index, axis=0).reshape(1, -1, row_width)
        near_values = jnp.take(key_pool[1], one_index, axis=0).reshape(1, -1, row_width)
        return source_part(one_query[None], near_keys, near_values, head_count)

    near_max, near_total, near_sum = lax.map(near_block, (query_blocks, near_index))
    rand_count = random_blocks.shape[1]
    flat_ids = random_blocks.reshape(-1)
    entry_count = flat_ids.shape[0]
    slot_count = -(-entry_count // shards)
    owner_of = flat_ids // per_device
    within_of = flat_ids % per_device
    matches = (owner_of[:, None] == jnp.arange(shards, dtype=jnp.int32)[None, :]).astype(jnp.int32)
    earlier = jnp.cumsum(matches, axis=0) - matches
    rank_of = jnp.sum(earlier * matches, axis=1)
    slot_ids = jnp.arange(slot_count, dtype=jnp.int32)
    placed = (matches[:, :, None] == 1) & (rank_of[:, None, None] == slot_ids[None, None, :])
    wanted = jnp.sum(jnp.where(placed, within_of[:, None, None], 0), axis=0)
    pick_index = owner_of * slot_count + rank_of
    asked_for = lax.all_to_all(wanted, "seq", split_axis=0, concat_axis=0, tiled=True)
    offered = jnp.take(stacked_blocks, asked_for.reshape(-1), axis=1)
    arrived = lax.all_to_all(offered, "seq", split_axis=1, concat_axis=1, tiled=True)
    chosen = jnp.take(arrived, pick_index, axis=1)
    repeated = jnp.repeat(query_blocks, rand_count, axis=0)
    rand_max, rand_total, rand_sum = source_part(repeated, chosen[0], chosen[1], head_count)
    block_max = jnp.concatenate(
        [near_max, rand_max.reshape(per_device, rand_count, head_count, BLK)], axis=1
    )
    block_total = jnp.concatenate(
        [near_total, rand_total.reshape(per_device, rand_count, head_count, BLK)], axis=1
    )
    block_sum = jnp.concatenate(
        [near_sum, rand_sum.reshape(per_device, rand_count, BLK, row_width)], axis=1
    )
    merger = partial(merge_sources, head_count=head_count)
    attended = jax.vmap(merger)(block_max, block_total, block_sum).reshape(-1, row_width)
    row_squares = jnp.sum(attended * attended, axis=1)
    all_squares = lax.psum(row_squares, "head")
    inverse = lax.rsqrt(all_squares / D + 1e-06)
    return (attended * inverse[:, None] * norm_gain[None, :]).astype(jnp.bfloat16)


def solution(mesh):
    placed = (
        P("seq", "head"),
        P("seq", "head"),
        P("seq", "head"),
        P("seq", None),
        P("seq", None),
        P(),
        P("head"),
    )
    return jax.shard_map(
        body, mesh=mesh, in_specs=placed, out_specs=P("seq", "head"), check_vma=False
    )
```

profile of v0, /device:TPU:1, one launch (start us, length us, event | category | flops | bytes accessed | tf_op | source)
XLA Modules:
  0.0 824.8 jit_solution(14655703358234410824)
XLA Ops:
  1.9 19.6 %all-to-all-start = ((s32[64,1,1]{2,1,0:T(1,128)}), s32[64,1,1]{2,1,0:T(1,128)S(1)}, u32[]{:S(2)}, u32[]{:S(2)}) async-start(s32[64,1,1]{2,1,0:T(1,128)} %copy.55), calls=%async_computation | async-start | bytes 65536 | tf_op jit(solution)/shard_map/all_to_all | solution.py:93
  23.3 11.5 %all-to-all-done = s32[64,1,1]{2,1,0:T(1,128)S(1)} async-done(((s32[64,1,1]{2,1,0:T(1,128)}), s32[64,1,1]{2,1,0:T(1,128)S(1)}, u32[]{:S(2)}, u32[]{:S(2)}) %all-to-all-start) | async-done | bytes 288 | tf_op jit(solution)/shard_map/all_to_all | solution.py:93
  34.7 1.2 reduce.8
  36.0 5.3 gather_fusion.3
  41.3 7.5 select_bitcast_fusion
  48.7 5.9 all-to-all-start.1
  54.7 4.2 collective-permute-start
  59.0 2.2 collective-permute-start.1
  61.2 11.2 %collective-permute-start.2 = (bf16[2,256,512]{2,1,0:T(8,128)(2,1)S(1)}, bf16[2,256,512]{2,1,0:T(8,128)(2,1)}, u32[]{:S(2)}, u32[]{:S(2)}) collective-permute-start(bf16[2,256,512]{2,1,0:T(8,128)(2,1)S(1)} %pad_maximum_fusion.1), channel_id=1, source_target_pairs={{0,504},{8,0},{16,8},{24,16},{32,24},{40,32},{48,40},{56,48},{64,5... | collective-permute-start | bytes 1572872 | tf_op jit(solution)/shard_map/ppermute | solution.py:15
  72.4 1.9 collective-permute-start.3
  76.5 617.7 %all-reduce.1 = bf16[2,2,64,512]{3,2,0,1:T(8,128)(2,1)S(1)} all-reduce(f32[2,2,64,512]{3,2,0,1:T(8,128)S(1)} %select_bitcast_fusion.2), channel_id=1, replica_groups=mesh['seq'=64,'head'=8] {'seq'}, use_global_device_ids=true, to_apply=%region_0.1 | all-reduce | flops 131072 | bytes 786432 | tf_op jit(solution)/shard_map/psum | solution.py:63
  697.7 1.9 pad_maximum_fusion
  699.6 44.4 %while.14 = (s32[]{:T(128)}, f32[4,1,4,64]{3,2,1,0:T(4,128)S(1)}, f32[4,1,4,64]{3,2,1,0:T(4,128)S(1)}, f32[4,1,64,512]{3,0,2,1:T(4,128)}, bf16[4,64,512]{2,1,0:T...) while((s32[]{:T(128)}, f32[4,1,4,64]{3,2,1,0:T(4,128)S(1)}, ...), condition=%wide.region_4.6_spmd, body=%wide.region_1.5_spmd.sunk | while | flops 119734864 | bytes 22364576 | solution.py:79
  699.6 2.0 slice_bitcast_fusion.3
  701.6 1.5 gather_fusion.1
  703.8 1.4 broadcast_select_fusion.3
  706.7 3.6 dynamic_update_slice.16
  710.7 2.0 slice_bitcast_fusion.3
  712.7 1.5 gather_fusion.1
  714.9 1.4 broadcast_select_fusion.3
  717.8 3.6 dynamic_update_slice.16
  721.8 2.0 slice_bitcast_fusion.3
  723.8 1.5 gather_fusion.1
  726.0 1.4 broadcast_select_fusion.3
  728.9 3.6 dynamic_update_slice.16
  732.9 2.0 slice_bitcast_fusion.3
  734.9 1.5 gather_fusion.1
  737.1 1.4 broadcast_select_fusion.3
  740.0 3.6 dynamic_update_slice.16
  744.0 1.3 concatenate.23
  746.3 4.0 gather_fusion.4
  754.7 69.2 %psum.15 = f32[256]{0:T(256)S(1)} all-reduce(f32[256]{0:T(256)S(1)} %reduce_sum.74), channel_id=1, replica_groups=mesh['seq'=64,'head'=8] {'head'}, use_global_device_ids=true, to_apply=%region_14.16 | all-reduce | flops 256 | bytes 2048 | tf_op jit(solution)/shard_map/psum | solution.py:111
  (120 shorter events, 25.1 us)
Async XLA Ops:
  1.9 32.8 %all-to-all-start = ((s32[64,1,1]{2,1,0:T(1,128)}), s32[64,1,1]{2,1,0:T(1,128)S(1)}, u32[]{:S(2)}, u32[]{:S(2)}) async-start(s32[64,1,1]{2,1,0:T(1,128)} %copy.55), calls=%async_computation | async-start | bytes 65536 | tf_op jit(solution)/shard_map/all_to_all | solution.py:93
  48.7 5.9 copy-start.1
  48.7 5.9 copy-start.2
  48.7 25.6 %copy-start.5 = (s32[4,3]{1,0:T(4,128)S(1)}, s32[4,3]{1,0:T(4,128)}, u32[]{:S(2)}) copy-start(s32[4,3]{1,0:T(4,128)} %param.15) | copy-start | bytes 148
  48.7 25.7 %copy-start.4 = (bf16[256,512]{1,0:T(8,128)(2,1)S(1)}, bf16[256,512]{1,0:T(8,128)(2,1)}, u32[]{:S(2)}) copy-start(bf16[256,512]{1,0:T(8,128)(2,1)} %param.11) | copy-start | bytes 786436
  48.7 697.5 %all-to-all-start.1 = ((bf16[2,64,64,512]{3,2,0,1:T(8,128)(2,1)}), bf16[2,64,64,512]{3,2,0,1:T(8,128)(2,1)}, u32[]{:S(2)}, u32[]{:S(2)}) async-start(bf16[2,64,64,512]{3,2,0,1:T(8,128)(2,1)} %select_bitcast_fusion), calls=%async_computation.1 | async-start | bytes 16777216 | tf_op jit(solution)/shard_map/all_to_all | solution.py:95
  54.6 21.0 %copy-start.7 = (s32[4,12]{1,0:T(4,128)S(1)}, s32[4,12]{1,0:T(4,128)}, u32[]{:S(2)}) copy-start(s32[4,12]{1,0:T(4,128)} %param.14) | copy-start | bytes 580
  54.7 639.4 %collective-permute-start = (bf16[2,256,512]{2,1,0:T(8,128)(2,1)S(1)}, bf16[2,256,512]{2,1,0:T(8,128)(2,1)}, u32[]{:S(2)}, u32[]{:S(2)}) collective-permute-start(bf16[2,256,512]{2,1,0:T(8,128)(2,1)S(1)} %pad_maximum_fusion.1), channel_id=1, source_target_pairs={{0,16},{8,24},{16,32},{24,40},{32,48},{40,56},{48,64},{56,72},{64,... | collective-permute-start | bytes 1572872 | tf_op jit(solution)/shard_map/ppermute | solution.py:15
  59.0 636.2 %collective-permute-start.1 = (bf16[2,256,512]{2,1,0:T(8,128)(2,1)S(1)}, bf16[2,256,512]{2,1,0:T(8,128)(2,1)}, u32[]{:S(2)}, u32[]{:S(2)}) collective-permute-start(bf16[2,256,512]{2,1,0:T(8,128)(2,1)S(1)} %pad_maximum_fusion.1), channel_id=1, source_target_pairs={{0,8},{8,16},{16,24},{24,32},{32,40},{40,48},{48,56},{56,64},{64,7... | collective-permute-start | bytes 1572872 | tf_op jit(solution)/shard_map/ppermute | solution.py:15
  61.2 635.2 %collective-permute-start.2 = (bf16[2,256,512]{2,1,0:T(8,128)(2,1)S(1)}, bf16[2,256,512]{2,1,0:T(8,128)(2,1)}, u32[]{:S(2)}, u32[]{:S(2)}) collective-permute-start(bf16[2,256,512]{2,1,0:T(8,128)(2,1)S(1)} %pad_maximum_fusion.1), channel_id=1, source_target_pairs={{0,504},{8,0},{16,8},{24,16},{32,24},{40,32},{48,40},{56,48},{64,5... | collective-permute-start | bytes 1572872 | tf_op jit(solution)/shard_map/ppermute | solution.py:15
  72.4 625.0 %collective-permute-start.3 = (bf16[2,256,512]{2,1,0:T(8,128)(2,1)S(1)}, bf16[2,256,512]{2,1,0:T(8,128)(2,1)S(1)}, u32[]{:S(2)}, u32[]{:S(2)}) collective-permute-start(bf16[2,256,512]{2,1,0:T(8,128)(2,1)S(1)} %pad_maximum_fusion.1), channel_id=1, source_target_pairs={{0,496},{8,504},{16,0},{24,8},{32,16},{40,24},{48,32},{56,40},{64,... | collective-permute-start | bytes 1572872 | tf_op jit(solution)/shard_map/ppermute | solution.py:15
  750.6 1.1 copy-start
  752.3 1.0 copy-start.3
  753.1 70.8 %copy-start.6 = (f32[512]{0:T(512)S(1)}, f32[512]{0:T(512)}, u32[]{:S(2)}) copy-start(f32[512]{0:T(512)} %param.17) | copy-start | bytes 6148
where the time goes:
time: 826 us; the launch traced here: 825 us
  blocking collectives  687 us (83%)
  local copies, waits for them, and re-layouts  53.4 us (6%)
  starting transfers between devices  45 us (5%)
  other arithmetic  22.4 us (3%)
  waiting for transfers between devices  11.5 us (1%)
    psum x1, blocking collectives, body(): global_kv = lax.psum(masked, 'seq').astype(jnp.bfloat16)  618 us
    psum x1, blocking collectives, body(): all_squares = lax.psum(row_squares, 'head')  69.2 us
    ppermute x4, starting transfers between devices, from_behind(): lax.ppermute(shard, axis, [(i, (i + by) % peers) for i in range(peers)])  19.6 us
    all_to_all x1, starting transfers between devices, body(): lax.all_to_all(wanted, 'seq', split_axis=0, concat_axis=0, tiled=True)  19.6 us
  transfers between devices with their start and end apart: 6, of which 1 were waited for; matrix products, arithmetic and copies ran while one was open for 7% of the time, Pallas kernels for 0%

commit v1 on v0

v1 whole, which is shorter than its diff:
```python
from functools import partial

import jax
import jax.numpy as jnp
from jax import lax
from jax.experimental import pallas as pl
from jax.experimental.pallas import tpu as pltpu
from jax.sharding import PartitionSpec as P

HD = 128
D = 4096
BLK = 64
NX, NY, NZ = 4, 8, 2
SHARDS = NX * NY * NZ
PER = 4
RANDS = 12
SLOTS = 14
HALF = 7
WIN = 12
MESH = pl.DeviceIdType.MESH


def exchange_kernel(ids_ref, k_ref, v_ref, near_ref, sel_ref,
                    key_col, value_col, out_buf, in_buf, ids_all, ids_smem,
                    own_sem, id_send, id_recv, z_send, z_recv, w_send, w_recv,
                    y_send, y_recv, x_send, x_recv, smem_sem):
    s = lax.axis_index("seq")
    mx = lax.rem(s, NX)
    my = lax.rem(s // NX, NY)
    mz = s // (NX * NY)
    kv = (k_ref, v_ref)
    col = (key_col, value_col)

    def at(z, y, x):
        return z * (NX * NY) + y * NX + x

    def wrap(value, size):
        return lax.rem(value + 2 * size, size)

    z_peer = at(1 - mz, my, mx)
    y_peer = (at(mz, wrap(my + 1, NY), mx), at(mz, wrap(my - 1, NY), mx))
    x_peer = [at(mz, my, wrap(mx + i, NX)) for i in range(NX)]
    w_peer = {o: wrap(s + o, SHARDS) for o in (-2, -1, 1, 2)}

    def remote(src, dst, send, recv, to):
        return pltpu.make_async_remote_copy(
            src_ref=src, dst_ref=dst, send_sem=send, recv_sem=recv,
            device_id={"seq": to}, device_id_type=MESH)

    barrier = pltpu.get_barrier_semaphore()
    greeted = [z_peer, *y_peer, *x_peer[1:], *w_peer.values()]
    for peer in greeted:
        pl.semaphore_signal(barrier, inc=1, device_id={"seq": peer}, device_id_type=MESH)
    own = [pltpu.make_async_copy(kv[c], col[c].at[0, my], own_sem.at[c]) for c in range(2)]
    own_ids = pltpu.make_async_copy(ids_ref, ids_all.at[mx], own_sem.at[2])
    for copy in own:
        copy.start()
    own_ids.start()
    pl.semaphore_wait(barrier, len(greeted))

    sends = []

    def y_copy(zz, c, way, t, y_src):
        part = pl.ds(0, PER) if t < 4 else pl.ds(2 * way, 2)
        block = col[c].at[zz, y_src, part]
        if t == 1 and zz == 0:
            source = kv[c]
        else:
            source = block
        return remote(source, block, y_send.at[zz, c, way, t - 1],
                      y_recv.at[zz, c, way, t - 1], y_peer[way])

    def y_start(zz, c, t):
        for way, sign in ((0, 1), (1, -1)):
            copy = y_copy(zz, c, way, t, wrap(my - sign * (t - 1), NY))
            copy.start()
            sends.append(copy)

    def y_wait(zz, c, t, way):
        sign = 1 - 2 * way
        y_copy(zz, c, way, t, wrap(my - sign * t, NY)).wait_recv()

    z_copies = [remote(kv[c], col[c].at[1, my], z_send.at[c], z_recv.at[c], z_peer)
                for c in range(2)]

    def y_phase(zz, c, t):
        if t == 0:
            if zz == 1:
                z_copies[c].wait_recv()
            y_start(zz, c, 1)
        elif t < 4:
            for way in range(2):
                y_wait(zz, c, t, way)
            y_start(zz, c, t + 1)
        else:
            for way in range(2):
                y_wait(zz, c, 4, way)

    def x_copy(c, way, i):
        to = x_peer[1] if way == 0 else x_peer[3]
        return remote(out_buf.at[c, way, i], in_buf.at[c, way, i], x_send.at[c, way, i],
                      x_recv.at[c, way, i], to)

    def x_phase(c, i):
        for way in range(2):
            away = (3 - i) if way == 0 else (1 + i)
            dest = wrap(mx + away, NX)
            if i == 3:
                dest = mx
            if i > 0:
                x_copy(c, way, i - 1).wait_recv()

            def fill(j, carry, way=way, dest=dest):
                slot = j + way * HALF
                block_id = ids_smem[dest, 0, slot]
                shard = block_id // PER
                picked = col[c][jnp.where(shard // (NX * NY) == mz, 0, 1),
                                lax.rem(shard // NX, NY), lax.rem(block_id, PER)]
                if i > 0:
                    mine = lax.rem(shard, NX) == mx
                    picked = lax.select(mine, picked, in_buf[c, way, i - 1, j])
                if i == 3:
                    sel_ref[c, slot] = picked
                else:
                    out_buf[c, way, i, j] = picked
                return carry

            lax.fori_loop(0, HALF, fill, 0)
            if i < 3:
                copy = x_copy(c, way, i)
                copy.start()
                sends.append(copy)

    y_phase(0, 0, 0)
    for copy in z_copies:
        copy.start()
    own_ids.wait()
    id_copies = []
    for i in (1, 2, 3):
        copy = remote(ids_ref, ids_all.at[mx], id_send.at[i - 1], id_recv.at[i - 1], x_peer[i])
        copy.start()
        id_copies.append(copy)
    near_copies = []
    for n, o in enumerate((1, -1, 2, -2)):
        for c in range(2):
            copy = remote(kv[c], near_ref.at[2 - o, c], w_send.at[n, c], w_recv.at[n, c], w_peer[o])
            copy.start()
            near_copies.append(copy)
    for copy in own:
        copy.wait()
    keep_own = [pltpu.make_async_copy(col[c].at[0, my], near_ref.at[2, c], own_sem.at[3 + c])
                for c in range(2)]
    for copy in keep_own:
        copy.start()

    begin = {(0, 0): 0, (1, 0): 3, (0, 1): 6, (1, 1): 9}
    x_at = {8: (0, 0), 9: (0, 1), 11: (0, 2), 13: (0, 3)}
    for tick in range(1, 14):
        for (zz, c), first in begin.items():
            t = tick - first
            if 0 <= t <= 4:
                y_phase(zz, c, t)
        if tick == 7:
            for i in (1, 2, 3):
                remote(ids_ref, ids_all.at[wrap(mx - i, NX)], id_send.at[i - 1],
                       id_recv.at[i - 1], x_peer[i]).wait_recv()
            to_smem = pltpu.make_async_copy(ids_all, ids_smem, smem_sem)
            to_smem.start()
            to_smem.wait()
        if tick in x_at:
            x_phase(*x_at[tick])
    for i in range(4):
        x_phase(1, i)

    for copy in keep_own:
        copy.wait()
    for copy in near_copies:
        copy.wait_recv()
    for copy in near_copies + id_copies + z_copies + sends:
        copy.wait_send()


def exchange(ids, keys, values):
    width = keys.shape[-1]
    dma = pltpu.SemaphoreType.DMA
    hbm = pl.BlockSpec(memory_space=pl.ANY)
    vmem = pl.BlockSpec(memory_space=pltpu.VMEM)
    return pl.pallas_call(
        exchange_kernel,
        out_shape=(jax.ShapeDtypeStruct((5, 2, PER, BLK, width), jnp.bfloat16),
                   jax.ShapeDtypeStruct((2, SLOTS, BLK, width), jnp.bfloat16)),
        in_specs=[vmem, hbm, hbm],
        out_specs=(hbm, vmem),
        scratch_shapes=[
            pltpu.VMEM((2, NY, PER, BLK, width), jnp.bfloat16),
            pltpu.VMEM((2, NY, PER, BLK, width), jnp.bfloat16),
            pltpu.VMEM((2, 2, 3, HALF, BLK, width), jnp.bfloat16),
            pltpu.VMEM((2, 2, 3, HALF, BLK, width), jnp.bfloat16),
            pltpu.VMEM((NX, 8, 128), jnp.int32),
            pltpu.SMEM((NX, 8, 128), jnp.int32),
            dma((5,)), dma((3,)), dma((3,)), dma((2,)), dma((2,)), dma((4, 2)), dma((4, 2)),
            dma((2, 2, 2, 4)), dma((2, 2, 2, 4)), dma((2, 2, 3)), dma((2, 2, 3)), dma(()),
        ],
        compiler_params=pltpu.CompilerParams(
            collective_id=0, has_side_effects=True, vmem_limit_bytes=48 << 20),
        name="exchange",
    )(ids, keys, values)


def attend_kernel(win_ref, q_ref, near_ref, sel_ref, out_ref, key_buf, value_buf):
    b = pl.program_id(0)
    s = lax.axis_index("seq")
    for j in range(WIN):
        block_id = win_ref[b, j]
        o = lax.rem(block_id // PER - s + 2 + SHARDS, SHARDS)
        w = lax.rem(block_id, PER)
        rows = pl.ds(j * BLK, BLK)
        key_buf[rows, :] = near_ref[o, 0, w]
        value_buf[rows, :] = near_ref[o, 1, w]
    for r in range(5):
        slot = b * 3 + r if r < 3 else RANDS + r - 3
        rows = pl.ds((WIN + r) * BLK, BLK)
        key_buf[rows, :] = sel_ref[0, slot]
        value_buf[rows, :] = sel_ref[1, slot]
    for h in range(q_ref.shape[-1] // HD):
        lanes = slice(h * HD, (h + 1) * HD)
        scores = lax.dot_general(q_ref[0, :, lanes], key_buf[:, lanes], (((1,), (1,)), ((), ())),
                                 preferred_element_type=jnp.float32)
        peak = jnp.max(scores, axis=-1, keepdims=True)
        lifted = jnp.exp((scores - peak) * HD ** -0.5)
        total = jnp.sum(lifted, axis=-1, keepdims=True)
        part = jnp.dot(lifted.astype(jnp.bfloat16), value_buf[:, lanes],
                       preferred_element_type=jnp.float32)
        out_ref[0, :, lanes] = part / total


def attend(window, queries, near, sel):
    width = queries.shape[-1]
    keys_total = (WIN + 5) * BLK
    whole = lambda shape: pl.BlockSpec(shape, lambda b, *_: (0,) * len(shape),
                                       pipeline_mode=pl.Buffered(1))
    return pl.pallas_call(
        attend_kernel,
        out_shape=jax.ShapeDtypeStruct((PER, BLK, width), jnp.float32),
        grid_spec=pltpu.PrefetchScalarGridSpec(
            num_scalar_prefetch=1, grid=(PER,),
            in_specs=[pl.BlockSpec((1, BLK, width), lambda b, *_: (b, 0, 0)),
                      whole(near.shape), whole(sel.shape)],
            out_specs=pl.BlockSpec((1, BLK, width), lambda b, *_: (b, 0, 0)),
            scratch_shapes=[pltpu.VMEM((keys_total, width), jnp.bfloat16),
                            pltpu.VMEM((keys_total, width), jnp.bfloat16)]),
        compiler_params=pltpu.CompilerParams(vmem_limit_bytes=48 << 20),
        name="attend",
    )(window, queries, near, sel)


def body(queries, key_rows, value_rows, window, random_blocks, global_blocks, norm_gain):
    width = queries.shape[1]
    blocks = lambda rows: rows.reshape(PER, BLK, width)
    ids = jnp.concatenate([random_blocks.reshape(-1), global_blocks])
    ids = jnp.broadcast_to(jnp.pad(ids, (0, 128 - SLOTS))[None, :], (8, 128))
    near, sel = exchange(ids, blocks(key_rows), blocks(value_rows))
    attended = attend(window, blocks(queries), near, sel).reshape(-1, width)
    row_squares = jnp.sum(attended * attended, axis=1)
    all_squares = lax.psum(row_squares, "head")
    inverse = lax.rsqrt(all_squares / D + 1e-06)
    return (attended * inverse[:, None] * norm_gain[None, :]).astype(jnp.bfloat16)


def solution(mesh):
    placed = (
        P("seq", "head"),
        P("seq", "head"),
        P("seq", "head"),
        P("seq", None),
        P("seq", None),
        P(),
        P("head"),
    )
    return jax.shard_map(
        body, mesh=mesh, in_specs=placed, out_specs=P("seq", "head"), check_vma=False
    )
```

time: 826 us -> 219 us (0.27)
  blocking collectives: 687 us -> 22.3 us
  Pallas kernels: 0 us -> 189 us
  local copies, waits for them, and re-layouts: 53.4 us -> 4.38 us
  starting transfers between devices: 45 us -> 0 us
  other arithmetic: 22.4 us -> 1.68 us
  waiting for transfers between devices: 11.5 us -> 0 us
    psum x1 -> x0, blocking collectives: 618 us -> none  [body(): global_kv = lax.psum(masked, 'seq').astype(jnp.bfloat16)]
    pallas_call x0 -> x2, Pallas kernels: none -> 189 us  [the longest x1 182 us: exchange(): pl.pallas_call(exchange_kernel, out_shape=(jax.ShapeDtypeStruct((5, 2, PE...]
    psum x1, blocking collectives: 69.2 us -> 22.3 us  [body(): all_squares = lax.psum(row_squares, 'head')]
    all_to_all x2 -> x0, starting transfers between devices: 25.5 us -> none  [the longest x1 19.6 us: body(): lax.all_to_all(wanted, 'seq', split_axis=0, concat_axis=0, tiled=True)]
    ppermute x4 -> x0, starting transfers between devices: 19.6 us -> none  [from_behind(): lax.ppermute(shard, axis, [(i, (i + by) % peers) for i in range(peers)])]
    gather x11 -> x0, local copies, waits for them, and re-layouts: 18.4 us -> none  [the longest x4 6.17 us: near_block(): jnp.take(key_pool[0], one_index, axis=0).reshape(1, -1, row_width)]
    dynamic_update_slice x8 -> x0, local copies, waits for them, and re-layouts: 14.6 us -> none  [body(): lax.map(near_block, (query_blocks, near_index))]
    select_n x10 -> x0, other arithmetic: 13.5 us -> none  [the longest x2 7.47 us: body(): offered = jnp.take(stacked_blocks, asked_for.reshape(-1), axis=1)]
  transfers between devices with their start and end apart: 6 -> 0, of which waited for: 1 -> 0; matrix products, arithmetic and copies ran while one was open for 7% -> 0% of each run, Pallas kernels for 0% -> 0%
where the time goes in v1:
time: 219 us; the launch traced here: 218 us
  Pallas kernels  189 us (86%)
  blocking collectives  22.3 us (10%)
  local copies, waits for them, and re-layouts  4.38 us (2%)
    pallas_call x1, Pallas kernels, exchange(): pl.pallas_call(exchange_kernel, out_shape=(jax.ShapeDtypeStruct((5, 2, PE...  182 us
    psum x1, blocking collectives, body(): all_squares = lax.psum(row_squares, 'head')  22.3 us
    pallas_call x1, Pallas kernels, attend(): pl.pallas_call(attend_kernel, out_shape=jax.ShapeDtypeStruct((PER, BLK, w...  7.02 us

profile of v1, /device:TPU:1, one launch (start us, length us, event | category | flops | bytes accessed | tf_op | source)
XLA Modules:
  0.0 217.8 jit_solution(325891285191927974)
XLA Ops:
  0.0 0.8 reshape.20
  0.8 0.7 pad_add_fusion
  1.5 0.0 copy-start.1
  1.5 0.9 copy-done.1
  2.5 0.0 copy-start.2
  2.5 0.9 copy-done.2
  3.4 182.4 %exchange.1 = (bf16[5,2,4,64,512]{4,3,2,1,0:T(8,128)(2,1)S(1)}, bf16[2,14,64,512]{3,2,1,0:T(8,128)(2,1)S(1)}) custom-call(s32[8,128]{1,0:T(8,128)S(1)} %broadcast_in_dim.2.ids_ref, bf16[4,64,512]{2,1,0:T(8,128)(2,1)S(1)} %bitcast.10, bf16[4,64,512]{2,1,0:T(8,128)(2,1)S(1)} %bitcast.11), custom_call_target="tpu_custom_call" | custom-call | tf_op jit(solution)/shard_map/exchange/pallas_call | solution.py:188
  185.8 0.0 copy-start
  185.8 0.9 copy-done
  186.8 0.0 copy-start.3
  186.8 0.7 copy-done.3
  187.4 0.0 copy-start.4
  187.5 7.0 %attend.1 = f32[4,64,512]{2,1,0:T(8,128)S(1)} custom-call(s32[4,12]{1,0:T(4,128)S(1)} %copy-done.3, bf16[4,64,512]{2,1,0:T(8,128)(2,1)S(1)} %bitcast.9, bf16[5,2,4,64,512]{4,3,2,1,0:T(8,128)(2,1)S(1)} %get-tuple-element.7.near_ref, bf16[2,14,64,512]{3,2,1,0:T(8,128)(2,1)S(1)} %get-tuple-element.8.sel_ref), custom_call_target="tpu_custom_call" | custom-call | tf_op jit(solution)/shard_map/attend/pallas_call | solution.py:242
  194.5 0.1 multiply_reduce_fusion
  194.6 0.1 reduce_sum.12
  194.7 22.3 %psum.7 = f32[256]{0:T(256)S(1)} all-reduce(f32[256]{0:T(256)S(1)} %reduce_sum.12), channel_id=1, replica_groups=mesh['seq'=64,'head'=8] {'head'}, use_global_device_ids=true, to_apply=%region_1.2 | all-reduce | flops 256 | bytes 2048 | tf_op jit(solution)/shard_map/psum | solution.py:265
  217.0 0.0 copy-done.4
  217.0 0.8 fusion.1
  (3 shorter events, 0.0 us)
Async XLA Ops:
  1.5 0.9 copy-start.1
  2.5 0.9 copy-start.2
  185.8 1.0 copy-start
  186.8 0.7 copy-start.3
  187.4 29.6 %copy-start.4 = (f32[512]{0:T(512)S(1)}, f32[512]{0:T(512)}, u32[]{:S(2)}) copy-start(f32[512]{0:T(512)} %param.13) | copy-start | bytes 6148

commit v2 on v1

v2 whole, which is shorter than its diff:
```python
from functools import partial

import jax
import jax.numpy as jnp
from jax import lax
from jax.experimental import pallas as pl
from jax.experimental.pallas import tpu as pltpu
from jax.sharding import PartitionSpec as P

HD = 128
D = 4096
BLK = 64
NX, NY, NZ = 4, 8, 2
SHARDS = NX * NY * NZ
PER = 4
RANDS = 12
SLOTS = 14
HALF = 7
WIN = 12
SPLIT = 2
GROUPS = 2 * SPLIT
LANES = 512 // SPLIT
FIRST, X_LAG, X_GAP = 3, 5, 2
MESH = pl.DeviceIdType.MESH


def remote_copy(src, dst, send, recv, axis, to):
    return pltpu.make_async_remote_copy(
        src_ref=src, dst_ref=dst, send_sem=send, recv_sem=recv,
        device_id={axis: to}, device_id_type=MESH)


def greet(axis, peers):
    barrier = pltpu.get_barrier_semaphore()
    for peer in peers:
        pl.semaphore_signal(barrier, inc=1, device_id={axis: peer}, device_id_type=MESH)
    return lambda: pl.semaphore_wait(barrier, len(peers))


def exchange_kernel(ids_ref, k_ref, v_ref, near_ref, sel_ref, *scratch):
    col = scratch[:GROUPS]
    (out_buf, in_buf, ids_all, ids_smem, own_sem, keep_sem, id_send, id_recv, z_send, z_recv,
     w_send, w_recv, y_send, y_recv, x_send, x_recv, smem_sem) = scratch[GROUPS:]
    s = lax.axis_index("seq")
    mx = lax.rem(s, NX)
    my = lax.rem(s // NX, NY)
    mz = s // (NX * NY)
    remote = partial(remote_copy, axis="seq")

    def lanes(g):
        return pl.ds((g % SPLIT) * LANES, LANES)

    own_kv = [(k_ref, v_ref)[g // SPLIT].at[:, :, lanes(g)] for g in range(GROUPS)]

    def at(z, y, x):
        return z * (NX * NY) + y * NX + x

    def wrap(value, size):
        return lax.rem(value + 2 * size, size)

    z_peer = at(1 - mz, my, mx)
    y_peer = (at(mz, wrap(my + 1, NY), mx), at(mz, wrap(my - 1, NY), mx))
    x_peer = [at(mz, my, wrap(mx + i, NX)) for i in range(NX)]

    await_peers = greet("seq", [z_peer, *y_peer, *x_peer[1:]])
    own = [pltpu.make_async_copy(own_kv[g], col[g].at[0, my], own_sem.at[g]) for g in range(GROUPS)]
    own_ids = pltpu.make_async_copy(ids_ref, ids_all.at[mx], smem_sem.at[0])
    for copy in own:
        copy.start()
    own_ids.start()
    await_peers()

    sends = []

    def begin(copy):
        copy.start()
        sends.append(copy)

    def y_copy(zz, g, way, t, y_src):
        part = pl.ds(0, PER) if t < 4 else pl.ds(2 * way, 2)
        block = col[g].at[zz, y_src, part]
        source = own_kv[g] if t == 1 and zz == 0 else block
        return remote(source, block, y_send.at[zz, g, way, t - 1],
                      y_recv.at[zz, g, way, t - 1], to=y_peer[way])

    def y_start(zz, g, t):
        for way, sign in ((0, 1), (1, -1)):
            begin(y_copy(zz, g, way, t, wrap(my - sign * (t - 1), NY)))

    def y_wait(zz, g, t):
        for way, sign in ((0, 1), (1, -1)):
            y_copy(zz, g, way, t, wrap(my - sign * t, NY)).wait_recv()

    z_copies = [remote(own_kv[g], col[g].at[1, my], z_send.at[g], z_recv.at[g], to=z_peer)
                for g in range(GROUPS)]

    def y_phase(zz, g, t):
        if t == 0:
            if zz == 1:
                z_copies[g].wait_recv()
        else:
            y_wait(zz, g, t)
        if t < 4:
            y_start(zz, g, t + 1)

    def w_copy(g, n):
        away, o = ((1, -1), (-1, 1), (2, 2), (2, -2))[n]
        to = x_peer[away % NX]
        shard = wrap(to + o, SHARDS)
        block = col[g].at[jnp.where(shard // (NX * NY) == mz, 0, 1), lax.rem(shard // NX, NY)]
        return remote(block, near_ref.at[o + 2, g // SPLIT, :, :, lanes(g)],
                      w_send.at[g, n], w_recv.at[g, n], to=to)

    def x_copy(g, way, i):
        return remote(out_buf.at[g, way, i], in_buf.at[g, way, i], x_send.at[g, way, i],
                      x_recv.at[g, way, i], to=x_peer[1] if way == 0 else x_peer[3])

    def x_phase(g, i):
        for way in range(2):
            dest = mx if i == 3 else wrap(mx + ((3 - i) if way == 0 else (1 + i)), NX)
            if i > 0:
                x_copy(g, way, i - 1).wait_recv()

            def fill(j, carry):
                slot = j + way * HALF
                block_id = ids_smem[dest, 0, slot]
                shard = block_id // PER
                picked = col[g][jnp.where(shard // (NX * NY) == mz, 0, 1),
                                lax.rem(shard // NX, NY), lax.rem(block_id, PER)]
                if i > 0:
                    mine = lax.rem(shard, NX) == mx
                    picked = lax.select(mine, picked, in_buf[g, way, i - 1, j])
                if i == 3:
                    sel_ref[g // SPLIT, slot, :, lanes(g)] = picked
                else:
                    out_buf[g, way, i, j] = picked
                return carry

            lax.fori_loop(0, HALF, fill, 0)
            if i < 3:
                begin(x_copy(g, way, i))

    y_phase(0, 0, 0)
    for copy in z_copies:
        begin(copy)
    own_ids.wait()
    for i in (1, 2, 3):
        begin(remote(ids_ref, ids_all.at[mx], id_send.at[i - 1], id_recv.at[i - 1], to=x_peer[i]))
    keep_own = []
    for g in range(GROUPS):
        own[g].wait()
        copy = pltpu.make_async_copy(col[g].at[0, my], near_ref.at[2, g // SPLIT, :, :, lanes(g)],
                                     keep_sem.at[g])
        copy.start()
        keep_own.append(copy)

    first = {(zz, g): FIRST * (2 * g + zz) for g in range(GROUPS) for zz in range(2)}
    w_at = {first[1, g] + 1: g for g in range(GROUPS)}
    x_at = {}
    for g in range(GROUPS):
        for i in range(4):
            x_at.setdefault(first[1, g] + X_LAG + X_GAP * i, []).append((g, i))
    for tick in range(1, max(x_at) + 1):
        for (zz, g), start in first.items():
            if 0 <= tick - start <= 4:
                y_phase(zz, g, tick - start)
        if tick in w_at:
            for n in range(4):
                begin(w_copy(w_at[tick], n))
        if tick == first[1, 0] + 4:
            for i in (1, 2, 3):
                remote(ids_ref, ids_all.at[wrap(mx - i, NX)], id_send.at[i - 1],
                       id_recv.at[i - 1], to=x_peer[i]).wait_recv()
            to_smem = pltpu.make_async_copy(ids_all, ids_smem, smem_sem.at[1])
            to_smem.start()
            to_smem.wait()
        for g, i in x_at.get(tick, ()):
            x_phase(g, i)

    for copy in keep_own:
        copy.wait()
    for g in range(GROUPS):
        for n in range(4):
            w_copy(g, n).wait_recv()
    for copy in sends:
        copy.wait_send()


def exchange(ids, keys, values):
    width = keys.shape[-1]
    dma = pltpu.SemaphoreType.DMA
    hbm = pl.BlockSpec(memory_space=pl.ANY)
    vmem = pl.BlockSpec(memory_space=pltpu.VMEM)
    return pl.pallas_call(
        exchange_kernel,
        out_shape=(jax.ShapeDtypeStruct((5, 2, PER, BLK, width), jnp.bfloat16),
                   jax.ShapeDtypeStruct((2, SLOTS, BLK, width), jnp.bfloat16)),
        in_specs=[vmem, hbm, hbm],
        out_specs=(hbm, vmem),
        scratch_shapes=[pltpu.VMEM((2, NY, PER, BLK, LANES), jnp.bfloat16)] * GROUPS + [
            pltpu.VMEM((GROUPS, 2, 3, HALF, BLK, LANES), jnp.bfloat16),
            pltpu.VMEM((GROUPS, 2, 3, HALF, BLK, LANES), jnp.bfloat16),
            pltpu.VMEM((NX, 8, 128), jnp.int32),
            pltpu.SMEM((NX, 8, 128), jnp.int32),
            dma((GROUPS,)), dma((GROUPS,)), dma((3,)), dma((3,)), dma((GROUPS,)), dma((GROUPS,)),
            dma((GROUPS, 4)), dma((GROUPS, 4)),
            dma((2, GROUPS, 2, 4)), dma((2, GROUPS, 2, 4)),
            dma((GROUPS, 2, 3)), dma((GROUPS, 2, 3)), dma((2,)),
        ],
        compiler_params=pltpu.CompilerParams(
            collective_id=0, has_side_effects=True, vmem_limit_bytes=48 << 20),
        name="exchange",
    )(ids, keys, values)


def attend_kernel(win_ref, q_ref, near_ref, sel_ref, out_ref, square_ref, key_buf, value_buf):
    b = pl.program_id(0)
    s = lax.axis_index("seq")
    for j in range(WIN):
        block_id = win_ref[b, j]
        o = lax.rem(block_id // PER - s + 2 + SHARDS, SHARDS)
        w = lax.rem(block_id, PER)
        rows = pl.ds(j * BLK, BLK)
        key_buf[rows, :] = near_ref[o, 0, w]
        value_buf[rows, :] = near_ref[o, 1, w]
    for r in range(5):
        slot = b * 3 + r if r < 3 else RANDS + r - 3
        rows = pl.ds((WIN + r) * BLK, BLK)
        key_buf[rows, :] = sel_ref[0, slot]
        value_buf[rows, :] = sel_ref[1, slot]
    squares = jnp.zeros(square_ref.shape[1:], jnp.float32)
    for h in range(q_ref.shape[-1] // HD):
        lanes = slice(h * HD, (h + 1) * HD)
        scores = lax.dot_general(q_ref[0, :, lanes], key_buf[:, lanes], (((1,), (1,)), ((), ())),
                                 preferred_element_type=jnp.float32)
        peak = jnp.max(scores, axis=-1, keepdims=True)
        lifted = jnp.exp((scores - peak) * HD ** -0.5)
        total = jnp.sum(lifted, axis=-1, keepdims=True)
        part = jnp.dot(lifted.astype(jnp.bfloat16), value_buf[:, lanes],
                       preferred_element_type=jnp.float32)
        attended = part / total
        squares += attended * attended
        out_ref[0, :, lanes] = attended
    square_ref[0] = squares


def attend(window, queries, near, sel):
    width = queries.shape[-1]
    keys_total = (WIN + 5) * BLK
    whole = lambda shape: pl.BlockSpec(shape, lambda b, *_: (0,) * len(shape),
                                       pipeline_mode=pl.Buffered(1))
    return pl.pallas_call(
        attend_kernel,
        out_shape=(jax.ShapeDtypeStruct((PER, BLK, width), jnp.float32),
                   jax.ShapeDtypeStruct((PER, BLK, HD), jnp.float32)),
        grid_spec=pltpu.PrefetchScalarGridSpec(
            num_scalar_prefetch=1, grid=(PER,),
            in_specs=[pl.BlockSpec((1, BLK, width), lambda b, *_: (b, 0, 0)),
                      whole(near.shape), whole(sel.shape)],
            out_specs=(pl.BlockSpec((1, BLK, width), lambda b, *_: (b, 0, 0)),
                       pl.BlockSpec((1, BLK, HD), lambda b, *_: (b, 0, 0))),
            scratch_shapes=[pltpu.VMEM((keys_total, width), jnp.bfloat16),
                            pltpu.VMEM((keys_total, width), jnp.bfloat16)]),
        compiler_params=pltpu.CompilerParams(vmem_limit_bytes=48 << 20),
        name="attend",
    )(window, queries, near, sel)


def norm_kernel(heads, attended_ref, square_ref, gain_ref, out_ref, sums, send_sem, recv_sem):
    me = lax.axis_index("head")
    peers = [lax.rem(me + i, heads) for i in range(1, heads)]
    await_peers = greet("head", peers)
    sums[me] = lax.dot_general(
        jnp.ones((8, HD), jnp.float32), square_ref[...], (((1,), (1,)), ((), ())),
        precision=lax.Precision.HIGHEST, preferred_element_type=jnp.float32)
    await_peers()
    copies = [remote_copy(sums.at[me], sums.at[me], send_sem.at[i], recv_sem.at[i], "head", peer)
              for i, peer in enumerate(peers)]
    for copy in copies:
        copy.start()
    for i in range(heads - 1):
        source = lax.rem(me + heads - 1 - i, heads)
        remote_copy(sums.at[source], sums.at[source], send_sem.at[i], recv_sem.at[i], "head",
                    peers[i]).wait_recv()
    total = sums[0]
    for i in range(1, heads):
        total += sums[i]
    inverse = jnp.transpose(lax.rsqrt(total / D + 1e-06))[:, :1]
    out_ref[...] = (attended_ref[...] * inverse * gain_ref[...]).astype(out_ref.dtype)
    for copy in copies:
        copy.wait_send()


def norm(attended, squares, gain):
    heads = lax.axis_size("head")
    dma = pltpu.SemaphoreType.DMA((heads - 1,))
    vmem = pl.BlockSpec(memory_space=pltpu.VMEM)
    return pl.pallas_call(
        partial(norm_kernel, heads),
        out_shape=jax.ShapeDtypeStruct(attended.shape, jnp.bfloat16),
        in_specs=[vmem] * 3,
        out_specs=vmem,
        scratch_shapes=[pltpu.VMEM((heads, 8, attended.shape[0]), jnp.float32), dma, dma],
        compiler_params=pltpu.CompilerParams(collective_id=1, has_side_effects=True),
        name="norm",
    )(attended, squares, gain)


def body(queries, key_rows, value_rows, window, random_blocks, global_blocks, norm_gain):
    width = queries.shape[1]
    blocks = lambda rows: rows.reshape(PER, BLK, width)
    ids = jnp.concatenate([random_blocks.reshape(-1), global_blocks])
    ids = jnp.broadcast_to(jnp.pad(ids, (0, 128 - SLOTS))[None, :], (8, 128))
    near, sel = exchange(ids, blocks(key_rows), blocks(value_rows))
    attended, squares = attend(window, blocks(queries), near, sel)
    return norm(attended.reshape(-1, width), squares.reshape(-1, HD), norm_gain[None, :])


def solution(mesh):
    placed = (
        P("seq", "head"),
        P("seq", "head"),
        P("seq", "head"),
        P("seq", None),
        P("seq", None),
        P(),
        P("head"),
    )
    return jax.shard_map(
        body, mesh=mesh, in_specs=placed, out_specs=P("seq", "head"), check_vma=False
    )
```

time: 219 us -> 199 us (0.909)
  blocking collectives: 22.3 us -> 0 us
  local copies, waits for them, and re-layouts: 4.38 us -> 7.41 us
    pallas_call x1 -> x2, Pallas kernels: 7.02 us -> 34.4 us  [the longest x1 27.4 us: norm(): pl.pallas_call(partial(norm_kernel, heads), out_shape=jax.ShapeDtypeStruc...]
    pallas_call x1, Pallas kernels: 182 us -> 156 us  [exchange(): pl.pallas_call(exchange_kernel, out_shape=(jax.ShapeDtypeStruct((5, 2, PE...]
    psum x1 -> x0, blocking collectives: 22.3 us -> none  [body(): all_squares = lax.psum(row_squares, 'head')]
    unnamed x10 -> x13, local copies, waits for them, and re-layouts: 3.53 us -> 6.63 us
where the time goes in v2:
time: 199 us; the launch traced here: 198 us
  Pallas kernels  190 us (95%)
  local copies, waits for them, and re-layouts  7.41 us (4%)
    pallas_call x1, Pallas kernels, exchange(): pl.pallas_call(exchange_kernel, out_shape=(jax.ShapeDtypeStruct((5, 2, PE...  156 us
    pallas_call x1, Pallas kernels, norm(): pl.pallas_call(partial(norm_kernel, heads), out_shape=jax.ShapeDtypeStruc...  27.4 us
    pallas_call x1, Pallas kernels, attend(): pl.pallas_call(attend_kernel, out_shape=(jax.ShapeDtypeStruct((PER, BLK,...  7.01 us
    unnamed x13, local copies, waits for them, and re-layouts  6.63 us

profile of v2, /device:TPU:1, one launch (start us, length us, event | category | flops | bytes accessed | tf_op | source)
XLA Modules:
  0.0 198.4 jit_solution(12081197094941749637)
XLA Ops:
  0.0 0.8 reshape.20
  0.8 0.7 pad_add_fusion
  1.5 0.0 copy-start.2
  1.5 0.9 copy-done.2
  2.5 0.0 copy-start.3
  2.5 0.9 copy-done.3
  3.4 155.8 %exchange.1 = (bf16[5,2,4,64,512]{4,3,2,1,0:T(8,128)(2,1)S(1)}, bf16[2,14,64,512]{3,2,1,0:T(8,128)(2,1)S(1)}) custom-call(s32[8,128]{1,0:T(8,128)S(1)} %broadcast_in_dim.4.ids_ref, bf16[4,64,512]{2,1,0:T(8,128)(2,1)S(1)} %bitcast.8, bf16[4,64,512]{2,1,0:T(8,128)(2,1)S(1)} %bitcast.9), custom_call_target="tpu_custom_call" | custom-call | tf_op jit(solution)/shard_map/exchange/pallas_call | solution.py:194
  159.3 0.0 copy-start.1
  159.3 0.9 copy-done.1
  160.2 0.0 copy-start.5
  160.2 0.7 copy-done.5
  160.9 7.0 %attend.1 = (f32[4,64,512]{2,1,0:T(8,128)S(1)}, f32[4,64,128]{2,1,0:T(8,128)S(1)}) custom-call(s32[4,12]{1,0:T(4,128)S(1)} %copy-done.5, bf16[4,64,512]{2,1,0:T(8,128)(2,1)S(1)} %bitcast.7, bf16[5,2,4,64,512]{4,3,2,1,0:T(8,128)(2,1)S(1)} %get-tuple-element.9.near_ref, bf16[2,14,64,512]{3,2,1,0:T(8,128)(2,1)S(1)} %get-tuple-element.10.sel_ref), custom_call_target="tpu_custom_call" | custom-call | tf_op jit(solution)/shard_map/attend/pallas_call | solution.py:252
  167.9 0.0 copy-start
  167.9 0.8 copy-done
  168.7 0.0 copy-start.4
  168.7 0.7 copy-done.4
  169.4 27.4 %norm.1 = bf16[256,512]{1,0:T(8,128)(2,1)} custom-call(f32[256,512]{1,0:T(8,128)} %bitcast.6, f32[256,128]{1,0:T(8,128)} %bitcast.10, f32[1,512]{1,0:T(1,128)} %bitcast.11), custom_call_target="tpu_custom_call" | custom-call | tf_op jit(solution)/shard_map/norm/pallas_call | solution.py:298
  196.8 1.7 copy.9
  (2 shorter events, 0.0 us)
Async XLA Ops:
  1.5 0.9 copy-start.2
  2.5 0.9 copy-start.3
  159.3 1.0 copy-start.1
  160.2 0.7 copy-start.5
  167.9 0.8 copy-start
  168.7 0.7 copy-start.4

commit v3 on v2

--- a/solution.py
+++ b/solution.py
@@ -17,10 +17,9 @@
 SLOTS = 14
 HALF = 7
 WIN = 12
-SPLIT = 2
-GROUPS = 2 * SPLIT
-LANES = 512 // SPLIT
-FIRST, X_LAG, X_GAP = 3, 5, 2
+PARTS = ((0, 0, 128), (0, 128, 256), (0, 384, 128), (1, 0, 256), (1, 256, 256))
+GROUPS = len(PARTS)
+PERIOD, EARLY, NEAR_AT, X_GAP = 3, 2, 1, 2
 MESH = pl.DeviceIdType.MESH
 
 
@@ -39,8 +38,9 @@
 
 def exchange_kernel(ids_ref, k_ref, v_ref, near_ref, sel_ref, *scratch):
     col = scratch[:GROUPS]
-    (out_buf, in_buf, ids_all, ids_smem, own_sem, keep_sem, id_send, id_recv, z_send, z_recv,
-     w_send, w_recv, y_send, y_recv, x_send, x_recv, smem_sem) = scratch[GROUPS:]
+    out_buf, in_buf = scratch[GROUPS:2 * GROUPS], scratch[2 * GROUPS:3 * GROUPS]
+    (ids_all, ids_smem, own_sem, keep_sem, id_send, id_recv, z_send, z_recv,
+     w_send, w_recv, y_send, y_recv, x_send, x_recv, smem_sem) = scratch[3 * GROUPS:]
     s = lax.axis_index("seq")
     mx = lax.rem(s, NX)
     my = lax.rem(s // NX, NY)
@@ -48,9 +48,9 @@
     remote = partial(remote_copy, axis="seq")
 
     def lanes(g):
-        return pl.ds((g % SPLIT) * LANES, LANES)
-
-    own_kv = [(k_ref, v_ref)[g // SPLIT].at[:, :, lanes(g)] for g in range(GROUPS)]
+        return pl.ds(PARTS[g][1], PARTS[g][2])
+
+    own_kv = [(k_ref, v_ref)[PARTS[g][0]].at[:, :, lanes(g)] for g in range(GROUPS)]
 
     def at(z, y, x):
         return z * (NX * NY) + y * NX + x
@@ -95,11 +95,7 @@
                 for g in range(GROUPS)]
 
     def y_phase(zz, g, t):
-        if t == 0:
-            if zz == 1:
-                z_copies[g].wait_recv()
-        else:
-            y_wait(zz, g, t)
+        y_wait(zz, g, t)
         if t < 4:
             y_start(zz, g, t + 1)
 
@@ -108,11 +104,11 @@
         to = x_peer[away % NX]
         shard = wrap(to + o, SHARDS)
         block = col[g].at[jnp.where(shard // (NX * NY) == mz, 0, 1), lax.rem(shard // NX, NY)]
-        return remote(block, near_ref.at[o + 2, g // SPLIT, :, :, lanes(g)],
+        return remote(block, near_ref.at[o + 2, PARTS[g][0], :, :, lanes(g)],
                       w_send.at[g, n], w_recv.at[g, n], to=to)
 
     def x_copy(g, way, i):
-        return remote(out_buf.at[g, way, i], in_buf.at[g, way, i], x_send.at[g, way, i],
+        return remote(out_buf[g].at[way, i], in_buf[g].at[way, i], x_send.at[g, way, i],
                       x_recv.at[g, way, i], to=x_peer[1] if way == 0 else x_peer[3])
 
     def x_phase(g, i):
@@ -129,45 +125,53 @@
                                 lax.rem(shard // NX, NY), lax.rem(block_id, PER)]
                 if i > 0:
                     mine = lax.rem(shard, NX) == mx
-                    picked = lax.select(mine, picked, in_buf[g, way, i - 1, j])
+                    picked = lax.select(mine, picked, in_buf[g][way, i - 1, j])
                 if i == 3:
-                    sel_ref[g // SPLIT, slot, :, lanes(g)] = picked
+                    sel_ref[PARTS[g][0], slot, :, lanes(g)] = picked
                 else:
-                    out_buf[g, way, i, j] = picked
+                    out_buf[g][way, i, j] = picked
                 return carry
 
             lax.fori_loop(0, HALF, fill, 0)
             if i < 3:
                 begin(x_copy(g, way, i))
 
-    y_phase(0, 0, 0)
-    for copy in z_copies:
-        begin(copy)
+    for g in range(GROUPS):
+        if g * PERIOD <= EARLY:
+            y_start(0, g, 1)
+        begin(z_copies[g])
     own_ids.wait()
     for i in (1, 2, 3):
         begin(remote(ids_ref, ids_all.at[mx], id_send.at[i - 1], id_recv.at[i - 1], to=x_peer[i]))
     keep_own = []
     for g in range(GROUPS):
         own[g].wait()
-        copy = pltpu.make_async_copy(col[g].at[0, my], near_ref.at[2, g // SPLIT, :, :, lanes(g)],
+        copy = pltpu.make_async_copy(col[g].at[0, my], near_ref.at[2, PARTS[g][0], :, :, lanes(g)],
                                      keep_sem.at[g])
         copy.start()
         keep_own.append(copy)
 
-    first = {(zz, g): FIRST * (2 * g + zz) for g in range(GROUPS) for zz in range(2)}
-    w_at = {first[1, g] + 1: g for g in range(GROUPS)}
     x_at = {}
     for g in range(GROUPS):
         for i in range(4):
-            x_at.setdefault(first[1, g] + X_LAG + X_GAP * i, []).append((g, i))
-    for tick in range(1, max(x_at) + 1):
-        for (zz, g), start in first.items():
-            if 0 <= tick - start <= 4:
-                y_phase(zz, g, tick - start)
-        if tick in w_at:
-            for n in range(4):
-                begin(w_copy(w_at[tick], n))
-        if tick == first[1, 0] + 4:
+            x_at.setdefault(PERIOD * g + 4 + X_GAP * i, []).append((g, i))
+    for tick in range(max(x_at) + 1):
+        for g in range(GROUPS):
+            start = max(0, PERIOD * g - EARLY)
+            if tick == start:
+                if start > 0:
+                    y_start(0, g, 1)
+                z_copies[g].wait_recv()
+                y_start(1, g, 1)
+        for g in range(GROUPS):
+            t = tick - PERIOD * g
+            if 1 <= t <= 4:
+                for zz in range(2):
+                    y_phase(zz, g, t)
+            if t == NEAR_AT:
+                for n in range(4):
+                    begin(w_copy(g, n))
+        if tick == 4:
             for i in (1, 2, 3):
                 remote(ids_ref, ids_all.at[wrap(mx - i, NX)], id_send.at[i - 1],
                        id_recv.at[i - 1], to=x_peer[i]).wait_recv()
@@ -197,9 +201,9 @@
                    jax.ShapeDtypeStruct((2, SLOTS, BLK, width), jnp.bfloat16)),
         in_specs=[vmem, hbm, hbm],
         out_specs=(hbm, vmem),
-        scratch_shapes=[pltpu.VMEM((2, NY, PER, BLK, LANES), jnp.bfloat16)] * GROUPS + [
-            pltpu.VMEM((GROUPS, 2, 3, HALF, BLK, LANES), jnp.bfloat16),
-            pltpu.VMEM((GROUPS, 2, 3, HALF, BLK, LANES), jnp.bfloat16),
+        scratch_shapes=[
+            *[pltpu.VMEM((2, NY, PER, BLK, part[2]), jnp.bfloat16) for part in PARTS],
+            *[pltpu.VMEM((2, 3, HALF, BLK, part[2]), jnp.bfloat16) for part in PARTS * 2],
             pltpu.VMEM((NX, 8, 128), jnp.int32),
             pltpu.SMEM((NX, 8, 128), jnp.int32),
             dma((GROUPS,)), dma((GROUPS,)), dma((3,)), dma((3,)), dma((GROUPS,)), dma((GROUPS,)),

time: 199 us -> 171 us (0.86)
  Pallas kernels: 190 us -> 163 us
    pallas_call x1, Pallas kernels: 156 us -> 130 us  [exchange(): pl.pallas_call(exchange_kernel, out_shape=(jax.ShapeDtypeStruct((5, 2, PE...]
where the time goes in v3:
time: 171 us
  Pallas kernels  163 us (95%)
  local copies, waits for them, and re-layouts  7.41 us (4%)
    pallas_call x1, Pallas kernels, exchange(): pl.pallas_call(exchange_kernel, out_shape=(jax.ShapeDtypeStruct((5, 2, PE...  130 us
    pallas_call x1, Pallas kernels, norm(): pl.pallas_call(partial(norm_kernel, heads), out_shape=jax.ShapeDtypeStruc...  26 us
    pallas_call x1, Pallas kernels, attend(): pl.pallas_call(attend_kernel, out_shape=(jax.ShapeDtypeStruct((PER, BLK,...  7.01 us
    unnamed x13, local copies, waits for them, and re-layouts  6.63 us

profile of v3, /device:TPU:1, one launch (start us, length us, event | category | flops | bytes accessed | tf_op | source)
XLA Modules:
  0.0 171.0 jit_solution(17842524790559351511)
XLA Ops:
  0.0 0.8 reshape.20
  0.8 0.7 pad_add_fusion
  1.5 0.0 copy-start.2
  1.5 0.9 copy-done.2
  2.5 0.0 copy-start.3
  2.5 0.9 copy-done.3
  3.4 129.8 %exchange.1 = (bf16[5,2,4,64,512]{4,3,2,1,0:T(8,128)(2,1)S(1)}, bf16[2,14,64,512]{3,2,1,0:T(8,128)(2,1)S(1)}) custom-call(s32[8,128]{1,0:T(8,128)S(1)} %broadcast_in_dim.4.ids_ref, bf16[4,64,512]{2,1,0:T(8,128)(2,1)S(1)} %bitcast.8, bf16[4,64,512]{2,1,0:T(8,128)(2,1)S(1)} %bitcast.9), custom_call_target="tpu_custom_call" | custom-call | tf_op jit(solution)/shard_map/exchange/pallas_call | solution.py:198
  133.2 0.0 copy-start.1
  133.2 0.9 copy-done.1
  134.2 0.0 copy-start.5
  134.2 0.7 copy-done.5
  134.8 7.0 %attend.1 = (f32[4,64,512]{2,1,0:T(8,128)S(1)}, f32[4,64,128]{2,1,0:T(8,128)S(1)}) custom-call(s32[4,12]{1,0:T(4,128)S(1)} %copy-done.5, bf16[4,64,512]{2,1,0:T(8,128)(2,1)S(1)} %bitcast.7, bf16[5,2,4,64,512]{4,3,2,1,0:T(8,128)(2,1)S(1)} %get-tuple-element.9.near_ref, bf16[2,14,64,512]{3,2,1,0:T(8,128)(2,1)S(1)} %get-tuple-element.10.sel_ref), custom_call_target="tpu_custom_call" | custom-call | tf_op jit(solution)/shard_map/attend/pallas_call | solution.py:256
  141.9 0.0 copy-start
  141.9 0.8 copy-done
  142.6 0.0 copy-start.4
  142.7 0.7 copy-done.4
  143.3 26.0 %norm.1 = bf16[256,512]{1,0:T(8,128)(2,1)} custom-call(f32[256,512]{1,0:T(8,128)} %bitcast.6, f32[256,128]{1,0:T(8,128)} %bitcast.10, f32[1,512]{1,0:T(1,128)} %bitcast.11), custom_call_target="tpu_custom_call" | custom-call | tf_op jit(solution)/shard_map/norm/pallas_call | solution.py:302
  169.4 1.7 copy.9
  (2 shorter events, 0.0 us)
Async XLA Ops:
  1.5 0.9 copy-start.2
  2.5 0.9 copy-start.3
  133.2 1.0 copy-start.1
  134.2 0.7 copy-start.5
  141.9 0.8 copy-start
  142.6 0.7 copy-start.4

commit v4 on v3

--- a/solution.py
+++ b/solution.py
@@ -217,65 +217,46 @@
     )(ids, keys, values)
 
 
-def attend_kernel(win_ref, q_ref, near_ref, sel_ref, out_ref, square_ref, key_buf, value_buf):
-    b = pl.program_id(0)
+def attend_kernel(heads, win_ref, q_ref, near_ref, sel_ref, gain_ref, out_ref,
+                  key_buf, value_buf, attended_buf, square_buf, sums, send_sem, recv_sem):
+    me = lax.axis_index("head")
     s = lax.axis_index("seq")
-    for j in range(WIN):
-        block_id = win_ref[b, j]
-        o = lax.rem(block_id // PER - s + 2 + SHARDS, SHARDS)
-        w = lax.rem(block_id, PER)
-        rows = pl.ds(j * BLK, BLK)
-        key_buf[rows, :] = near_ref[o, 0, w]
-        value_buf[rows, :] = near_ref[o, 1, w]
-    for r in range(5):
-        slot = b * 3 + r if r < 3 else RANDS + r - 3
-        rows = pl.ds((WIN + r) * BLK, BLK)
-        key_buf[rows, :] = sel_ref[0, slot]
-        value_buf[rows, :] = sel_ref[1, slot]
-    squares = jnp.zeros(square_ref.shape[1:], jnp.float32)
-    for h in range(q_ref.shape[-1] // HD):
-        lanes = slice(h * HD, (h + 1) * HD)
-        scores = lax.dot_general(q_ref[0, :, lanes], key_buf[:, lanes], (((1,), (1,)), ((), ())),
-                                 preferred_element_type=jnp.float32)
-        peak = jnp.max(scores, axis=-1, keepdims=True)
-        lifted = jnp.exp((scores - peak) * HD ** -0.5)
-        total = jnp.sum(lifted, axis=-1, keepdims=True)
-        part = jnp.dot(lifted.astype(jnp.bfloat16), value_buf[:, lanes],
-                       preferred_element_type=jnp.float32)
-        attended = part / total
-        squares += attended * attended
-        out_ref[0, :, lanes] = attended
-    square_ref[0] = squares
-
-
-def attend(window, queries, near, sel):
-    width = queries.shape[-1]
-    keys_total = (WIN + 5) * BLK
-    whole = lambda shape: pl.BlockSpec(shape, lambda b, *_: (0,) * len(shape),
-                                       pipeline_mode=pl.Buffered(1))
-    return pl.pallas_call(
-        attend_kernel,
-        out_shape=(jax.ShapeDtypeStruct((PER, BLK, width), jnp.float32),
-                   jax.ShapeDtypeStruct((PER, BLK, HD), jnp.float32)),
-        grid_spec=pltpu.PrefetchScalarGridSpec(
-            num_scalar_prefetch=1, grid=(PER,),
-            in_specs=[pl.BlockSpec((1, BLK, width), lambda b, *_: (b, 0, 0)),
-                      whole(near.shape), whole(sel.shape)],
-            out_specs=(pl.BlockSpec((1, BLK, width), lambda b, *_: (b, 0, 0)),
-                       pl.BlockSpec((1, BLK, HD), lambda b, *_: (b, 0, 0))),
-            scratch_shapes=[pltpu.VMEM((keys_total, width), jnp.bfloat16),
-                            pltpu.VMEM((keys_total, width), jnp.bfloat16)]),
-        compiler_params=pltpu.CompilerParams(vmem_limit_bytes=48 << 20),
-        name="attend",
-    )(window, queries, near, sel)
-
-
-def norm_kernel(heads, attended_ref, square_ref, gain_ref, out_ref, sums, send_sem, recv_sem):
-    me = lax.axis_index("head")
     peers = [lax.rem(me + i, heads) for i in range(1, heads)]
     await_peers = greet("head", peers)
+
+    def one_block(b, carry):
+        for j in range(WIN):
+            block_id = win_ref[b, j]
+            o = jnp.minimum(lax.rem(block_id // PER - s + 2 + SHARDS, SHARDS), 4)
+            w = lax.rem(block_id, PER)
+            rows = pl.ds(j * BLK, BLK)
+            key_buf[rows, :] = near_ref[o, 0, w]
+            value_buf[rows, :] = near_ref[o, 1, w]
+        for r in range(5):
+            slot = b * 3 + r if r < 3 else RANDS + r - 3
+            rows = pl.ds((WIN + r) * BLK, BLK)
+            key_buf[rows, :] = sel_ref[0, slot]
+            value_buf[rows, :] = sel_ref[1, slot]
+        squares = jnp.zeros((BLK, HD), jnp.float32)
+        for h in range(q_ref.shape[-1] // HD):
+            lanes = slice(h * HD, (h + 1) * HD)
+            scores = lax.dot_general(q_ref[b, :, lanes], key_buf[:, lanes], (((1,), (1,)), ((), ())),
+                                     preferred_element_type=jnp.float32)
+            peak = jnp.max(scores, axis=-1, keepdims=True)
+            lifted = jnp.exp((scores - peak) * HD ** -0.5)
+            total = jnp.sum(lifted, axis=-1, keepdims=True)
+            part = jnp.dot(lifted.astype(jnp.bfloat16), value_buf[:, lanes],
+                           preferred_element_type=jnp.float32)
+            attended = part / total
+            squares += attended * attended
+            attended_buf[b, :, lanes] = attended
+        square_buf[b] = squares
+        return carry
+
+    lax.fori_loop(0, PER, one_block, 0)
     sums[me] = lax.dot_general(
-        jnp.ones((8, HD), jnp.float32), square_ref[...], (((1,), (1,)), ((), ())),
+        jnp.ones((8, HD), jnp.float32), square_buf[...].reshape(PER * BLK, HD),
+        (((1,), (1,)), ((), ())),
         precision=lax.Precision.HIGHEST, preferred_element_type=jnp.float32)
     await_peers()
     copies = [remote_copy(sums.at[me], sums.at[me], send_sem.at[i], recv_sem.at[i], "head", peer)
@@ -290,24 +271,34 @@
     for i in range(1, heads):
         total += sums[i]
     inverse = jnp.transpose(lax.rsqrt(total / D + 1e-06))[:, :1]
-    out_ref[...] = (attended_ref[...] * inverse * gain_ref[...]).astype(out_ref.dtype)
+    for b in range(PER):
+        rows = slice(b * BLK, (b + 1) * BLK)
+        out_ref[rows, :] = (attended_buf[b] * inverse[rows] * gain_ref[...]).astype(out_ref.dtype)
     for copy in copies:
         copy.wait_send()
 
 
-def norm(attended, squares, gain):
+def attend(window, queries, near, sel, gain):
+    width = queries.shape[-1]
     heads = lax.axis_size("head")
+    keys_total = (WIN + 5) * BLK
     dma = pltpu.SemaphoreType.DMA((heads - 1,))
     vmem = pl.BlockSpec(memory_space=pltpu.VMEM)
     return pl.pallas_call(
-        partial(norm_kernel, heads),
-        out_shape=jax.ShapeDtypeStruct(attended.shape, jnp.bfloat16),
-        in_specs=[vmem] * 3,
+        partial(attend_kernel, heads),
+        out_shape=jax.ShapeDtypeStruct((PER * BLK, width), jnp.bfloat16),
+        in_specs=[pl.BlockSpec(memory_space=pltpu.SMEM)] + [vmem] * 4,
         out_specs=vmem,
-        scratch_shapes=[pltpu.VMEM((heads, 8, attended.shape[0]), jnp.float32), dma, dma],
-        compiler_params=pltpu.CompilerParams(collective_id=1, has_side_effects=True),
-        name="norm",
-    )(attended, squares, gain)
+        scratch_shapes=[
+            pltpu.VMEM((keys_total, width), jnp.bfloat16),
+            pltpu.VMEM((keys_total, width), jnp.bfloat16),
+            pltpu.VMEM((PER, BLK, width), jnp.float32),
+            pltpu.VMEM((PER, BLK, HD), jnp.float32),
+            pltpu.VMEM((heads, 8, PER * BLK), jnp.float32), dma, dma],
+        compiler_params=pltpu.CompilerParams(
+            collective_id=1, has_side_effects=True, vmem_limit_bytes=48 << 20),
+        name="attend",
+    )(window, queries, near, sel, gain)
 
 
 def body(queries, key_rows, value_rows, window, random_blocks, global_blocks, norm_gain):
@@ -316,8 +307,7 @@
     ids = jnp.concatenate([random_blocks.reshape(-1), global_blocks])
     ids = jnp.broadcast_to(jnp.pad(ids, (0, 128 - SLOTS))[None, :], (8, 128))
     near, sel = exchange(ids, blocks(key_rows), blocks(value_rows))
-    attended, squares = attend(window, blocks(queries), near, sel)
-    return norm(attended.reshape(-1, width), squares.reshape(-1, HD), norm_gain[None, :])
+    return attend(window, blocks(queries), near, sel, norm_gain[None, :])
 
 
 def solution(mesh):

time: 171 us -> 167 us (0.977)
  Pallas kernels: 163 us -> 160 us
  local copies, waits for them, and re-layouts: 7.41 us -> 5.68 us
    pallas_call x2 -> x1, Pallas kernels: 33.1 us -> 30.1 us  [attend(): pl.pallas_call(partial(attend_kernel, heads), out_shape=jax.ShapeDtypeStr...]
    unnamed x13 -> x11, local copies, waits for them, and re-layouts: 6.63 us -> 4.91 us
where the time goes in v4:
time: 167 us; the launch traced here: 166 us
  Pallas kernels  160 us (96%)
  local copies, waits for them, and re-layouts  5.68 us (3%)
    pallas_call x1, Pallas kernels, exchange(): pl.pallas_call(exchange_kernel, out_shape=(jax.ShapeDtypeStruct((5, 2, PE...  130 us
    pallas_call x1, Pallas kernels, attend(): pl.pallas_call(partial(attend_kernel, heads), out_shape=jax.ShapeDtypeStr...  30.1 us
    unnamed x11, local copies, waits for them, and re-layouts  4.91 us

profile of v4, /device:TPU:1, one launch (start us, length us, event | category | flops | bytes accessed | tf_op | source)
XLA Modules:
  0.0 166.3 jit_solution(12264784616919815736)
XLA Ops:
  0.0 0.8 reshape.14
  0.8 0.7 pad_add_fusion
  1.5 0.0 copy-start.1
  1.5 0.9 copy-done.1
  2.5 0.0 copy-start.2
  2.5 0.9 copy-done.2
  3.4 129.8 %exchange.1 = (bf16[5,2,4,64,512]{4,3,2,1,0:T(8,128)(2,1)S(1)}, bf16[2,14,64,512]{3,2,1,0:T(8,128)(2,1)S(1)}) custom-call(s32[8,128]{1,0:T(8,128)S(1)} %broadcast_in_dim.4.ids_ref, bf16[4,64,512]{2,1,0:T(8,128)(2,1)S(1)} %bitcast.5, bf16[4,64,512]{2,1,0:T(8,128)(2,1)S(1)} %bitcast.6), custom_call_target="tpu_custom_call" | custom-call | tf_op jit(solution)/shard_map/exchange/pallas_call | solution.py:198
  133.2 0.0 copy-start
  133.2 0.9 copy-done
  134.2 0.0 copy-start.3
  134.2 0.7 copy-done.3
  134.8 0.0 copy-start.4
  134.8 0.7 copy-done.4
  135.5 30.1 %attend.1 = bf16[256,512]{1,0:T(8,128)(2,1)S(1)} custom-call(s32[4,12]{1,0:T(4,128)S(1)} %copy-done.3, bf16[4,64,512]{2,1,0:T(8,128)(2,1)S(1)} %bitcast.4, bf16[5,2,4,64,512]{4,3,2,1,0:T(8,128)(2,1)S(1)} %get-tuple-element.7.near_ref, bf16[2,14,64,512]{3,2,1,0:T(8,128)(2,1)S(1)} %get-tuple-element.8.sel_ref, f32[1,512]{1,0:T(1,128)S(1)} %bitcast.7), custom_call_target="tpu_custom_call" | custom-call | tf_op jit(solution)/shard_map/attend/pallas_call | solution.py:287
  165.6 0.7 copy.9
  (2 shorter events, 0.0 us)
Async XLA Ops:
  1.5 0.9 copy-start.1
  2.5 0.9 copy-start.2
  133.2 1.0 copy-start
  134.2 0.7 copy-start.3
  134.8 0.7 copy-start.4

commit v5 on v4

--- a/solution.py
+++ b/solution.py
@@ -29,19 +29,23 @@
         device_id={axis: to}, device_id_type=MESH)
 
 
-def greet(axis, peers):
+def greet(seq_peers, head_peers):
     barrier = pltpu.get_barrier_semaphore()
+    peers = [{"seq": peer} for peer in seq_peers] + [{"head": peer} for peer in head_peers]
     for peer in peers:
-        pl.semaphore_signal(barrier, inc=1, device_id={axis: peer}, device_id_type=MESH)
+        pl.semaphore_signal(barrier, inc=1, device_id=peer, device_id_type=MESH)
     return lambda: pl.semaphore_wait(barrier, len(peers))
 
 
-def exchange_kernel(ids_ref, k_ref, v_ref, near_ref, sel_ref, *scratch):
+def exchange_kernel(heads, ids_ref, win_ref, k_ref, v_ref, q_ref, gain_ref, out_ref, *scratch):
     col = scratch[:GROUPS]
     out_buf, in_buf = scratch[GROUPS:2 * GROUPS], scratch[2 * GROUPS:3 * GROUPS]
     (ids_all, ids_smem, own_sem, keep_sem, id_send, id_recv, z_send, z_recv,
-     w_send, w_recv, y_send, y_recv, x_send, x_recv, smem_sem) = scratch[3 * GROUPS:]
+     w_send, w_recv, y_send, y_recv, x_send, x_recv, smem_sem, near_ref, sel_ref, key_buf, value_buf,
+     attended_buf, square_buf, peak_buf, total_buf, sums, head_send, head_recv) = scratch[3 * GROUPS:]
     s = lax.axis_index("seq")
+    me = lax.axis_index("head")
+    head_peers = [lax.rem(me + i, heads) for i in range(1, heads)]
     mx = lax.rem(s, NX)
     my = lax.rem(s // NX, NY)
     mz = s // (NX * NY)
@@ -62,7 +66,7 @@
     y_peer = (at(mz, wrap(my + 1, NY), mx), at(mz, wrap(my - 1, NY), mx))
     x_peer = [at(mz, my, wrap(mx + i, NX)) for i in range(NX)]
 
-    await_peers = greet("seq", [z_peer, *y_peer, *x_peer[1:]])
+    await_peers = greet([z_peer, *y_peer, *x_peer[1:]], head_peers)
     own = [pltpu.make_async_copy(own_kv[g], col[g].at[0, my], own_sem.at[g]) for g in range(GROUPS)]
     own_ids = pltpu.make_async_copy(ids_ref, ids_all.at[mx], smem_sem.at[0])
     for copy in own:
@@ -135,6 +139,48 @@
             lax.fori_loop(0, HALF, fill, 0)
             if i < 3:
                 begin(x_copy(g, way, i))
+
+    def softmax_part(b, count, h):
+        lanes_h = slice(h * HD, (h + 1) * HD)
+        scores = lax.dot_general(q_ref[b, :, lanes_h], key_buf[:count, lanes_h],
+                                 (((1,), (1,)), ((), ())), preferred_element_type=jnp.float32)
+        peak = jnp.max(scores, axis=-1, keepdims=True)
+        lifted = jnp.exp((scores - peak) * HD ** -0.5)
+        part = jnp.dot(lifted.astype(jnp.bfloat16), value_buf[:count, lanes_h],
+                       preferred_element_type=jnp.float32)
+        return peak, jnp.sum(lifted, axis=-1, keepdims=True), part
+
+    def window_part(b, carry):
+        for j in range(WIN):
+            block_id = win_ref[b, j]
+            o = jnp.minimum(lax.rem(block_id // PER - s + 2 + SHARDS, SHARDS), 4)
+            w = lax.rem(block_id, PER)
+            key_buf[pl.ds(j * BLK, BLK), :] = near_ref[o, 0, w]
+            value_buf[pl.ds(j * BLK, BLK), :] = near_ref[o, 1, w]
+        for h in range(q_ref.shape[-1] // HD):
+            peak, total, part = softmax_part(b, WIN * BLK, h)
+            peak_buf[b, h] = jnp.broadcast_to(peak, (BLK, HD))
+            total_buf[b, h] = jnp.broadcast_to(total, (BLK, HD))
+            attended_buf[b, :, h * HD:(h + 1) * HD] = part
+        return carry
+
+    def rest_part(b, carry):
+        for r in range(5):
+            slot = b * 3 + r if r < 3 else RANDS + r - 3
+            key_buf[pl.ds(r * BLK, BLK), :] = sel_ref[0, slot]
+            value_buf[pl.ds(r * BLK, BLK), :] = sel_ref[1, slot]
+        squares = jnp.zeros((BLK, HD), jnp.float32)
+        for h in range(q_ref.shape[-1] // HD):
+            peak, total, part = softmax_part(b, 5 * BLK, h)
+            overall = jnp.maximum(peak_buf[b, h], peak)
+            before = jnp.exp((peak_buf[b, h] - overall) * HD ** -0.5)
+            now = jnp.exp((peak - overall) * HD ** -0.5)
+            attended = (attended_buf[b, :, h * HD:(h + 1) * HD] * before + part * now) / (
+                total_buf[b, h] * before + total * now)
+            squares += attended * attended
+            attended_buf[b, :, h * HD:(h + 1) * HD] = attended
+        square_buf[b] = squares
+        return carry
 
     for g in range(GROUPS):
         if g * PERIOD <= EARLY:
@@ -180,27 +226,51 @@
             to_smem.wait()
         for g, i in x_at.get(tick, ()):
             x_phase(g, i)
-
-    for copy in keep_own:
-        copy.wait()
-    for g in range(GROUPS):
-        for n in range(4):
-            w_copy(g, n).wait_recv()
+        if tick == max(x_at) - 2 * X_GAP:
+            for copy in keep_own:
+                copy.wait()
+            for g in range(GROUPS):
+                for n in range(4):
+                    w_copy(g, n).wait_recv()
+            lax.fori_loop(0, 2, window_part, 0)
+        if tick == max(x_at) - X_GAP:
+            lax.fori_loop(2, PER, window_part, 0)
+
+    lax.fori_loop(0, PER, rest_part, 0)
+    sums[me] = lax.dot_general(
+        jnp.ones((8, HD), jnp.float32), square_buf[...].reshape(PER * BLK, HD),
+        (((1,), (1,)), ((), ())),
+        precision=lax.Precision.HIGHEST, preferred_element_type=jnp.float32)
+    for i, peer in enumerate(head_peers):
+        begin(remote_copy(sums.at[me], sums.at[me], head_send.at[i], head_recv.at[i], "head", peer))
+    for i in range(heads - 1):
+        source = lax.rem(me + heads - 1 - i, heads)
+        remote_copy(sums.at[source], sums.at[source], head_send.at[i], head_recv.at[i], "head",
+                    head_peers[i]).wait_recv()
+    total = sums[0]
+    for i in range(1, heads):
+        total += sums[i]
+    inverse = jnp.transpose(lax.rsqrt(total / D + 1e-06))[:, :1]
+    for b in range(PER):
+        rows = slice(b * BLK, (b + 1) * BLK)
+        out_ref[rows, :] = (attended_buf[b] * inverse[rows] * gain_ref[...]).astype(out_ref.dtype)
     for copy in sends:
         copy.wait_send()
 
 
-def exchange(ids, keys, values):
+def exchange(ids, window, keys, values, queries, gain):
     width = keys.shape[-1]
+    heads = lax.axis_size("head")
     dma = pltpu.SemaphoreType.DMA
     hbm = pl.BlockSpec(memory_space=pl.ANY)
     vmem = pl.BlockSpec(memory_space=pltpu.VMEM)
+    f32 = lambda *shape: pltpu.VMEM(shape, jnp.float32)
+    bf16 = lambda *shape: pltpu.VMEM(shape, jnp.bfloat16)
     return pl.pallas_call(
-        exchange_kernel,
-        out_shape=(jax.ShapeDtypeStruct((5, 2, PER, BLK, width), jnp.bfloat16),
-                   jax.ShapeDtypeStruct((2, SLOTS, BLK, width), jnp.bfloat16)),
-        in_specs=[vmem, hbm, hbm],
-        out_specs=(hbm, vmem),
+        partial(exchange_kernel, heads),
+        out_shape=jax.ShapeDtypeStruct((PER * BLK, width), jnp.bfloat16),
+        in_specs=[vmem, pl.BlockSpec(memory_space=pltpu.SMEM), hbm, hbm, vmem, vmem],
+        out_specs=vmem,
         scratch_shapes=[
             *[pltpu.VMEM((2, NY, PER, BLK, part[2]), jnp.bfloat16) for part in PARTS],
             *[pltpu.VMEM((2, 3, HALF, BLK, part[2]), jnp.bfloat16) for part in PARTS * 2],
@@ -210,95 +280,16 @@
             dma((GROUPS, 4)), dma((GROUPS, 4)),
             dma((2, GROUPS, 2, 4)), dma((2, GROUPS, 2, 4)),
             dma((GROUPS, 2, 3)), dma((GROUPS, 2, 3)), dma((2,)),
+            bf16(5, 2, PER, BLK, width), bf16(2, SLOTS, BLK, width),
+            bf16(WIN * BLK, width), bf16(WIN * BLK, width),
+            f32(PER, BLK, width), f32(PER, BLK, HD),
+            f32(PER, width // HD, BLK, HD), f32(PER, width // HD, BLK, HD),
+            f32(heads, 8, PER * BLK), dma((heads - 1,)), dma((heads - 1,)),
         ],
         compiler_params=pltpu.CompilerParams(
             collective_id=0, has_side_effects=True, vmem_limit_bytes=48 << 20),
         name="exchange",
-    )(ids, keys, values)
-
-
-def attend_kernel(heads, win_ref, q_ref, near_ref, sel_ref, gain_ref, out_ref,
-                  key_buf, value_buf, attended_buf, square_buf, sums, send_sem, recv_sem):
-    me = lax.axis_index("head")
-    s = lax.axis_index("seq")
-    peers = [lax.rem(me + i, heads) for i in range(1, heads)]
-    await_peers = greet("head", peers)
-
-    def one_block(b, carry):
-        for j in range(WIN):
-            block_id = win_ref[b, j]
-            o = jnp.minimum(lax.rem(block_id // PER - s + 2 + SHARDS, SHARDS), 4)
-            w = lax.rem(block_id, PER)
-            rows = pl.ds(j * BLK, BLK)
-            key_buf[rows, :] = near_ref[o, 0, w]
-            value_buf[rows, :] = near_ref[o, 1, w]
-        for r in range(5):
-            slot = b * 3 + r if r < 3 else RANDS + r - 3
-            rows = pl.ds((WIN + r) * BLK, BLK)
-            key_buf[rows, :] = sel_ref[0, slot]
-            value_buf[rows, :] = sel_ref[1, slot]
-        squares = jnp.zeros((BLK, HD), jnp.float32)
-        for h in range(q_ref.shape[-1] // HD):
-            lanes = slice(h * HD, (h + 1) * HD)
-            scores = lax.dot_general(q_ref[b, :, lanes], key_buf[:, lanes], (((1,), (1,)), ((), ())),
-                                     preferred_element_type=jnp.float32)
-            peak = jnp.max(scores, axis=-1, keepdims=True)
-            lifted = jnp.exp((scores - peak) * HD ** -0.5)
-            total = jnp.sum(lifted, axis=-1, keepdims=True)
-            part = jnp.dot(lifted.astype(jnp.bfloat16), value_buf[:, lanes],
-                           preferred_element_type=jnp.float32)
-            attended = part / total
-            squares += attended * attended
-            attended_buf[b, :, lanes] = attended
-        square_buf[b] = squares
-        return carry
-
-    lax.fori_loop(0, PER, one_block, 0)
-    sums[me] = lax.dot_general(
-        jnp.ones((8, HD), jnp.float32), square_buf[...].reshape(PER * BLK, HD),
-        (((1,), (1,)), ((), ())),
-        precision=lax.Precision.HIGHEST, preferred_element_type=jnp.float32)
-    await_peers()
-    copies = [remote_copy(sums.at[me], sums.at[me], send_sem.at[i], recv_sem.at[i], "head", peer)
-              for i, peer in enumerate(peers)]
-    for copy in copies:
-        copy.start()
-    for i in range(heads - 1):
-        source = lax.rem(me + heads - 1 - i, heads)
-        remote_copy(sums.at[source], sums.at[source], send_sem.at[i], recv_sem.at[i], "head",
-                    peers[i]).wait_recv()
-    total = sums[0]
-    for i in range(1, heads):
-        total += sums[i]
-    inverse = jnp.transpose(lax.rsqrt(total / D + 1e-06))[:, :1]
-    for b in range(PER):
-        rows = slice(b * BLK, (b + 1) * BLK)
-        out_ref[rows, :] = (attended_buf[b] * inverse[rows] * gain_ref[...]).astype(out_ref.dtype)
-    for copy in copies:
-        copy.wait_send()
-
-
-def attend(window, queries, near, sel, gain):
-    width = queries.shape[-1]
-    heads = lax.axis_size("head")
-    keys_total = (WIN + 5) * BLK
-    dma = pltpu.SemaphoreType.DMA((heads - 1,))
-    vmem = pl.BlockSpec(memory_space=pltpu.VMEM)
-    return pl.pallas_call(
-        partial(attend_kernel, heads),
-        out_shape=jax.ShapeDtypeStruct((PER * BLK, width), jnp.bfloat16),
-        in_specs=[pl.BlockSpec(memory_space=pltpu.SMEM)] + [vmem] * 4,
-        out_specs=vmem,
-        scratch_shapes=[
-            pltpu.VMEM((keys_total, width), jnp.bfloat16),
-            pltpu.VMEM((keys_total, width), jnp.bfloat16),
-            pltpu.VMEM((PER, BLK, width), jnp.float32),
-            pltpu.VMEM((PER, BLK, HD), jnp.float32),
-            pltpu.VMEM((heads, 8, PER * BLK), jnp.float32), dma, dma],
-        compiler_params=pltpu.CompilerParams(
-            collective_id=1, has_side_effects=True, vmem_limit_bytes=48 << 20),
-        name="attend",
-    )(window, queries, near, sel, gain)
+    )(ids, window, keys, values, queries, gain)
 
 
 def body(queries, key_rows, value_rows, window, random_blocks, global_blocks, norm_gain):
@@ -306,8 +297,8 @@
     blocks = lambda rows: rows.reshape(PER, BLK, width)
     ids = jnp.concatenate([random_blocks.reshape(-1), global_blocks])
     ids = jnp.broadcast_to(jnp.pad(ids, (0, 128 - SLOTS))[None, :], (8, 128))
-    near, sel = exchange(ids, blocks(key_rows), blocks(value_rows))
-    return attend(window, blocks(queries), near, sel, norm_gain[None, :])
+    return exchange(ids, window, blocks(key_rows), blocks(value_rows), blocks(queries),
+                    norm_gain[None, :])
 
 
 def solution(mesh):

time: 167 us -> 163 us (0.976)
  Pallas kernels: 160 us -> 157 us
    pallas_call x2 -> x1, Pallas kernels: 160 us -> 157 us  [exchange(): pl.pallas_call(partial(exchange_kernel, heads), out_shape=jax.ShapeDtypeS...]
    unnamed x11 -> x15, local copies, waits for them, and re-layouts: 4.91 us -> 5.5 us
where the time goes in v5:
time: 163 us
  Pallas kernels  157 us (96%)
  local copies, waits for them, and re-layouts  5.59 us (3%)
    pallas_call x1, Pallas kernels, exchange(): pl.pallas_call(partial(exchange_kernel, heads), out_shape=jax.ShapeDtypeS...  157 us
    unnamed x15, local copies, waits for them, and re-layouts  5.5 us

profile of v5, /device:TPU:1, one launch (start us, length us, event | category | flops | bytes accessed | tf_op | source)
XLA Modules:
  0.0 162.7 jit_solution(11881904521624874518)
XLA Ops:
  0.0 0.0 copy-start.5
  0.0 0.7 copy-done.5
  0.7 0.0 copy-start.6
  0.7 0.1 reshape.13
  0.8 0.6 copy-done.6
  1.3 0.1 pad_add_fusion
  1.4 0.0 copy-start.3
  1.4 0.0 copy-start.4
  1.4 0.7 copy-done.3
  2.1 0.0 copy-done.4
  2.1 0.0 copy-start
  2.1 0.9 copy-done
  3.1 0.0 copy-start.1
  3.1 0.9 copy-done.1
  4.0 0.0 copy-start.2
  4.0 0.9 copy-done.2
  5.0 157.0 %exchange.1 = bf16[256,512]{1,0:T(8,128)(2,1)S(1)} custom-call(s32[8,128]{1,0:T(8,128)S(1)} %broadcast_in_dim.4.ids_ref, s32[4,12]{1,0:T(4,128)S(1)} %copy-done.3, bf16[4,64,512]{2,1,0:T(8,128)(2,1)S(1)} %bitcast.4, bf16[4,64,512]{2,1,0:T(8,128)(2,1)S(1)} %bitcast.5, bf16[4,64,512]{2,1,0:T(8,128)(2,1)S(1)} %bitcast.6, f32[1,512]{1,0:T(1,128)S(1)} %bitcast.7), custom_call_target="tpu_custom_call" | custom-call | tf_op jit(solution)/shard_map/exchange/pallas_call | solution.py:269
  162.0 0.7 copy.9
  (2 shorter events, 0.0 us)
Async XLA Ops:
  0.0 0.7 copy-start.5
  0.7 0.7 copy-start.6
  1.4 0.7 copy-start.3
  1.4 0.7 copy-start.4
  2.1 0.9 copy-start
  3.1 0.9 copy-start.1
  4.0 0.9 copy-start.2
